TPU v7x, 32 devices: a whole 2x2x4 slice. The times are simulated.
32 devices in a mesh: rep: 2 (over y), seq: 4 (over z), tp: 2 (over x), sub: 2 (over core).
Axes of the slice: x: 2, y: 2, z: 4, core: 2. Of those that a mesh axis runs over, the one named last changes fastest.
Arguments:
- latents: bfloat16 [3072, 3072], P(('rep', 'seq')), parts along dimension 0, may hold values from -6 to 6
- w_qkv: bfloat16 [3072, 3, 24, 128], P('seq', None, ('tp', 'sub')), may hold values from -0.109375 to 0.109375
- w_out: bfloat16 [24, 128, 3072], P(('tp', 'sub'), None, 'seq'), may hold values from -0.15625 to 0.15625
- query_gain: float32 [128], replicated, may hold values from 1.5 to 20
- key_gain: float32 [128], replicated, may hold values from 1.5 to 20
- mod_shift: float32 [6144], P('rep'), parts along dimension 0, may hold values from -3 to 3
- mod_scale: float32 [6144], P('rep'), parts along dimension 0, may hold values from -0.5 to 0.5
- mod_gate: float32 [6144], P('rep'), parts along dimension 0, may hold values from 0.5 to 1.5
- block_list: int32 [8, 9], P(('rep', 'seq')), parts along dimension 0, may hold values from 0 to 3, as said below
- block_live: int32 [8, 9], P(('rep', 'seq')), parts along dimension 0, may hold values from 0 to 1, as said below
- key_valid: int32 [3072], P(('rep', 'seq')), parts along dimension 0, may hold values from 0 to 1, as said below
Outputs:
- block_out: bfloat16 [3072, 3072], P(('rep', 'seq'), ('tp', 'sub')), parts along dimension 0
There are 2 independent parts, one for each index of `rep`. A program takes and returns all parts, laid end to end along the dimension named above; an argument that names none is the same for every part. Nothing has to cross between parts.
Inputs may be any that keep to these rules, and one draw needn't show every extreme that they name: `block_list`: tiles are numbered frame by frame, 2 tiles to a frame of tiles. Row a lists, in a drawn order, the tiles within 1 frames of tiles and 1 tile column of tile a; entries outside the video or dropped have block_live 0, and those outside the video repeat a. Live entries are distinct, and a itself is always live. `block_live`: see block_list. `key_valid`: within each tile either all tokens are real or the last 144 are padding.
All inputs are finite; a program needn't handle non-finite values.
Results may differ from a plain program's by a relative error of at most 0.012.
The roundings to bfloat16 on the way count: a program that leaves them out, or rounds other values in their place, can miss the bound.
Values may be sent and summed in bfloat16 or wider, within the bound.
No kernel may reach another device: no remote copies, remote signals or barrier semaphores. Data moves between devices by JAX's collectives and lax.ppermute only.
A program may use at most 128 MiB of HBM per device.

v0:
```python
import math
import jax
import jax.numpy as jnp
from jax import lax
from jax.sharding import PartitionSpec as P

HD = 128
TILE = 384


def modulate(latents, mod_shift, mod_scale):
    x_float = latents.astype(jnp.float32)
    centre = x_float - jnp.mean(x_float, axis=-1, keepdims=True)
    spread = jnp.mean(centre * centre, axis=-1, keepdims=True)
    return (centre * lax.rsqrt(spread + 1e-06) * (1.0 + mod_scale) + mod_shift).astype(jnp.bfloat16)


def head_norm(raw_heads, gain):
    square = jnp.mean(raw_heads * raw_heads, axis=-1, keepdims=True)
    return (raw_heads * lax.rsqrt(square + 1e-06) * gain).astype(jnp.bfloat16)


def add_rows(normed, block_rows):
    return jnp.einsum("td,dshe->tshe", normed, block_rows, preferred_element_type=jnp.float32)


def attend_piece(queries, tile_rows, state_now, pieces):
    key_rows, value_rows, key_ok = pieces
    row_count = key_rows.shape[0]
    tile_of = jnp.arange(row_count, dtype=jnp.int32) // TILE
    one_hot = (tile_of[None, :] == jnp.arange(tile_rows.shape[1], dtype=jnp.int32)[:, None]).astype(
        jnp.bfloat16
    )
    allowed = (jnp.dot(tile_rows, one_hot, preferred_element_type=jnp.float32) > 0.5) & (
        key_ok[None, :] > 0
    )
    score_scale = 1.0 / math.sqrt(HD)
    old_peak, old_total, weighted = state_now
    scores = (
        jnp.einsum("qhe,khe->hqk", queries, key_rows, preferred_element_type=jnp.float32)
        * score_scale
    )
    masked = jnp.where(allowed[None], scores, -1e30)
    new_peak = jnp.maximum(old_peak, jnp.max(masked, axis=2))
    weights = jnp.where(allowed[None], jnp.exp(masked - new_peak[:, :, None]), 0.0)
    new_total = jnp.sum(weights, axis=2)
    added = jnp.einsum(
        "hqk,khe->qhe", weights.astype(jnp.bfloat16), value_rows, preferred_element_type=jnp.float32
    )
    return (new_peak, new_total, added)


def local(
    latents,
    w_qkv,
    w_out,
    query_gain,
    key_gain,
    mod_shift,
    mod_scale,
    mod_gate,
    block_list,
    block_live,
    key_valid,
):
    tok_rows = latents.shape[0]
    heads_here = w_qkv.shape[2]
    tiles_all = block_list.shape[0] * lax.axis_size("seq")
    normed = modulate(latents, mod_shift, mod_scale)
    qkv = add_rows(normed, lax.all_gather(w_qkv, "seq", axis=0, tiled=True))
    queries = head_norm(qkv[:, 0], query_gain)
    key_rows = head_norm(qkv[:, 1], key_gain)
    value_rows = qkv[:, 2].astype(jnp.bfloat16)
    tile_ids = jnp.arange(tiles_all, dtype=jnp.int32)
    tile_hits = jnp.any(
        (block_list[:, :, None] == tile_ids[None, None, :]) & (block_live[:, :, None] > 0), axis=1
    )
    tile_rows = jnp.repeat(tile_hits.astype(jnp.bfloat16), TILE, axis=0)
    start_state = (
        jnp.full((heads_here, tok_rows), -1e30, jnp.float32),
        jnp.zeros((heads_here, tok_rows), jnp.float32),
        jnp.zeros((tok_rows, heads_here, HD), jnp.float32),
    )
    final_peak, final_total, weighted = attend_piece(
        queries,
        tile_rows,
        start_state,
        (
            lax.all_gather(key_rows, "seq", axis=0, tiled=True),
            lax.all_gather(value_rows, "seq", axis=0, tiled=True),
            lax.all_gather(key_valid, "seq", axis=0, tiled=True),
        ),
    )
    attended = (weighted / jnp.transpose(final_total)[:, :, None]).astype(jnp.bfloat16)
    head_terms = jnp.einsum(
        "the,hec->tc",
        attended,
        lax.all_gather(w_out, "seq", axis=2, tiled=True),
        preferred_element_type=jnp.float32,
    )
    projected = lax.psum_scatter(
        head_terms.astype(jnp.bfloat16), ("tp", "sub"), scatter_dimension=1, tiled=True
    ).astype(jnp.float32)
    out_width = projected.shape[1]
    offset = lax.axis_index(("tp", "sub")) * out_width
    latent_cols = lax.dynamic_slice_in_dim(latents, offset, out_width, 1).astype(jnp.float32)
    gate_cols = lax.dynamic_slice_in_dim(mod_gate, offset, out_width, 0)
    return (latent_cols + gate_cols * projected).astype(jnp.bfloat16)


def solution(mesh):
    in_specs = (
        P(("rep", "seq"), None),
        P("seq", None, ("tp", "sub"), None),
        P(("tp", "sub"), None, "seq"),
        P(),
        P(),
        P("rep"),
        P("rep"),
        P("rep"),
        P(("rep", "seq"), None),
        P(("rep", "seq"), None),
        P(("rep", "seq")),
    )
    out_specs = P(("rep", "seq"), ("tp", "sub"))
    return jax.shard_map(local, mesh=mesh, in_specs=in_specs, out_specs=out_specs, check_vma=False)
```

profile of v0, /device:TPU:0, one launch (start us, length us, event | category | flops | bytes accessed | tf_op | source)
XLA Modules:
  0.0 515.9 jit_solution(16770260743124015059)
XLA Ops:
  6.5 0.0 all-gather.7.cloned.1.call-start
  6.5 6.0 %copy.22 = bf16[768,3,6,128]{0,3,2,1:T(8,128)(2,1)} copy(bf16[768,3,6,128]{3,0,2,1:T(8,128)(2,1)} %param.12) | data formatting | bytes 7077888 | tf_op args[1]
  12.6 0.0 copy-start.1
  12.6 0.0 copy-start.3
  12.6 0.0 copy-start.7
  12.6 0.0 all-gather.7.cloned.1.call-update
  12.6 0.0 all-gather.9.cloned.1.call-start
  12.7 1.6 copy-done.1
  14.3 0.4 convert_reduce_fusion
  14.6 0.8 fusion.8
  15.4 0.0 copy-done.3
  15.4 244.0 %all-gather.7.cloned.1.call-done = bf16[3072,3,6,128]{0,3,2,1:T(8,128)(2,1)} async-done(((bf16[768,3,6,128]{0,3,2,1:T(8,128)(2,1)}), bf16[3072,3,6,128]{0,3,2,1:T(8,128)(2,1)}) %all-gather.7.cloned.1.call-update) | async-done | bytes 14155792 | tf_op jit(solution)/shard_map/all_gather | solution.py:70
  259.4 0.0 copy-done.7
  259.4 0.0 copy-start.6
  259.4 10.7 %fusion.13 = f32[384,2304]{0,1:S(1)} fusion(bf16[3072,2304]{0,1:T(8,128)(2,1)} %bitcast.46, bf16[384,3072]{1,0:T(8,128)(2,1)S(1)} %copy-done.1, f32[3072]{0:T(1024)S(1)} %copy-done.7, f32[3072]{0:T(1024)S(1)} %broadcast_add_fusion, f32[384]{0:T(512)S(1)} %add_rsqrt_fusion.2, f32[384]{0:T(512)S(1)} %broadcast_multiply_fusion), kind=kOutput, calls=%fused_computation.18 | convolution fusion | flops 5442895872 | bytes 20081664
  270.1 0.0 copy-start.2
  270.1 0.0 copy-start.4
  270.1 0.0 copy-start.8
  270.1 0.0 copy-start.9
  270.1 0.2 multiply_reduce_fusion.1
  270.3 1.5 copy-done.2
  271.8 0.0 copy-done.6
  271.8 1.0 multiply_convert_fusion
  272.8 0.0 all-gather.9.cloned.1.call-update
  272.8 0.0 copy-start.5
  272.9 0.0 all-gather.11.cloned.1.call-start
  272.9 0.7 all-gather.11.cloned.1.call-update
  273.6 0.0 all-gather.13.cloned.1.call-start
  273.6 2.2 slice.28
  275.8 0.0 all-gather.13.cloned.1.call-update
  275.8 0.0 reduce-scatter.2.cloned.1.call-start
  275.9 0.0 copy-done.4
  275.9 12.4 %all-gather.1 = s32[4,1,384]{2,1,0:T(1,128)S(1)} all-gather(s32[1,1,384]{2,1,0:T(1,128)S(1)} %reshape.138), channel_id=1, replica_groups=mesh['rep'=2,'seq'=4,'tp'=2,'sub'=2] {'seq'}, dimensions={0}, use_global_device_ids=true | all-gather | bytes 7680 | tf_op jit(solution)/shard_map/all_gather | solution.py:91
  288.4 0.0 copy-done.8
  288.4 0.0 copy-done.9
  288.4 0.1 fusion.43
  288.5 0.5 fusion.12
  289.1 32.4 %all-gather.9.cloned.1.call-done = bf16[1536,6,128]{0,2,1:T(8,128)(2,1)} async-done(((bf16[384,6,128]{0,2,1:T(8,128)(2,1)}), bf16[1536,6,128]{0,2,1:T(8,128)(2,1)}) %all-gather.9.cloned.1.call-update) | async-done | bytes 2359312 | tf_op jit(solution)/shard_map/all_gather | solution.py:89
  321.5 0.0 copy-done.5
  321.5 5.0 fusion
  326.5 0.0 copy-start
  326.5 5.9 %copy-done = f32[6,384,1536]{2,1,0:T(8,128)} copy-done((f32[6,384,1536]{2,1,0:T(8,128)}, f32[6,384,1536]{2,1,0:T(8,128)S(1)}, u32[]{:S(2)}) %copy-start) | copy-done | bytes 14155800
  332.4 4.2 fusion.1
  336.6 74.5 %all-gather.11.cloned.1.call-done = bf16[6,128,3072]{2,1,0:T(8,128)(2,1)} async-done(((bf16[6,128,768]{2,1,0:T(8,128)(2,1)}), bf16[6,128,3072]{2,1,0:T(8,128)(2,1)}) %all-gather.11.cloned.1.call-update) | async-done | bytes 4718608 | tf_op jit(solution)/shard_map/all_gather | solution.py:98
  411.1 50.1 %all-gather.13.cloned.1.call-done = bf16[1536,1,6,128]{0,3,2,1:T(8,128)(2,1)} async-done(((bf16[384,1,6,128]{0,3,2,1:T(8,128)(2,1)}), bf16[1536,1,6,128]{0,3,2,1:T(8,128)(2,1)}) %all-gather.13.cloned.1.call-update) | async-done | bytes 2359312 | tf_op jit(solution)/shard_map/all_gather | solution.py:90
  461.2 14.5 %bitcast_convert_fusion = bf16[384,3072]{1,0:T(8,128)(2,1)} fusion(bf16[6,128,3072]{2,1,0:T(8,128)(2,1)} %all-gather.11.cloned.1.call-done, f32[6,384,1536]{2,1,0:T(8,128)} %copy-done, f32[6,384]{1,0:T(8,128)S(1)} %broadcast_maximum_fusion, pred[384,1536]{1,0:T(8,128)(4,1)S(1)} %fusion.12, bf16[1536,1,6,128]{0,3,2,1:T(8,128)(2,1)} %all-gather.13.cloned.1.call-done, ...), kind=kOutput, calls=%fused_computation.15 | convolution fusion | flops 2737373184 | bytes 24201216 | tf_op jit(solution)/shard_map/the,hec->tc/dot_general | solution.py:95
  475.7 0.0 reduce-scatter.2.cloned.1.call-update
  475.7 0.8 dynamic_slice.7
  476.5 30.8 %reduce-scatter.2.cloned.1.call-done = bf16[384,768]{1,0:T(8,128)(2,1)} async-done(((bf16[384,3072]{1,0:T(8,128)(2,1)}), bf16[384,768]{1,0:T(8,128)(2,1)}) %reduce-scatter.2.cloned.1.call-update) | async-done | bytes 589840 | tf_op jit(solution)/shard_map/reduce_scatter | solution.py:101
  507.3 2.1 add_convert_fusion
  (12 shorter events, 0.1 us)
Async XLA Ops:
  6.5 252.9 %all-gather.7.cloned.1.call-start = ((), (), s32[]{:S(2)}) async-start(), calls=%async_computation.1 | async-start | bytes 17694720 | tf_op jit(solution)/shard_map/all_gather | solution.py:70
  12.6 1.7 copy-start.1
  12.6 2.8 copy-start.3
  12.6 246.8 %copy-start.7 = (f32[3072]{0:T(1024)S(1)}, f32[3072]{0:T(1024)}, u32[]{:S(2)}) copy-start(f32[3072]{0:T(1024)} %param.16) | copy-start | bytes 36868
  12.6 308.9 %all-gather.9.cloned.1.call-start = ((), (), s32[]{:S(2)}) async-start(), calls=%async_computation.2 | async-start | bytes 2949120 | tf_op jit(solution)/shard_map/all_gather | solution.py:89
  259.4 12.4 %copy-start.6 = (f32[128]{0:T(128)S(1)}, f32[128]{0:T(128)}, u32[]{:S(2)}) copy-start(f32[128]{0:T(128)} %param.15) | copy-start | bytes 1540
  270.1 1.8 copy-start.2
  270.1 5.8 %copy-start.4 = (s32[384]{0:T(512)S(1)}, s32[384]{0:T(512)}, u32[]{:S(2)}) copy-start(s32[384]{0:T(512)} %param.21) | copy-start | bytes 4612
  270.1 18.3 %copy-start.8 = (s32[1,9]{1,0:T(1,128)S(1)}, s32[1,9]{1,0:T(1,128)}, u32[]{:S(2)}) copy-start(s32[1,9]{1,0:T(1,128)} %param.20) | copy-start | bytes 112
  270.1 18.3 %copy-start.9 = (s32[1,9]{1,0:T(1,128)S(1)}, s32[1,9]{1,0:T(1,128)}, u32[]{:S(2)}) copy-start(s32[1,9]{1,0:T(1,128)} %param.19) | copy-start | bytes 112
  272.8 48.6 %copy-start.5 = (f32[128]{0:T(128)S(1)}, f32[128]{0:T(128)}, u32[]{:S(2)}) copy-start(f32[128]{0:T(128)} %param.14) | copy-start | bytes 1540
  272.9 138.2 %all-gather.11.cloned.1.call-start = ((), (), s32[]{:S(2)}) async-start(), calls=%async_computation.3 | async-start | bytes 5898240 | tf_op jit(solution)/shard_map/all_gather | solution.py:98
  273.6 187.6 %all-gather.13.cloned.1.call-start = ((), (), s32[]{:S(2)}) async-start(), calls=%async_computation.5 | async-start | bytes 2949120 | tf_op jit(solution)/shard_map/all_gather | solution.py:90
  275.8 231.5 %reduce-scatter.2.cloned.1.call-start = ((), (), s32[]{:S(2)}) async-start(), calls=%async_computation.4 | async-start | bytes 2949120 | tf_op jit(solution)/shard_map/reduce_scatter | solution.py:101
  326.5 5.9 %copy-start = (f32[6,384,1536]{2,1,0:T(8,128)}, f32[6,384,1536]{2,1,0:T(8,128)S(1)}, u32[]{:S(2)}) copy-start(f32[6,384,1536]{2,1,0:T(8,128)S(1)} %get-tuple-element.8) | copy-start | bytes 42467332
Sparse Core Ops, SparseCore 0:
  12.7 246.6 all-gather.6
  273.0 48.4 all-gather.8
  323.0 87.9 all-gather.10
  412.5 48.6 all-gather.12
  475.8 31.4 reduce-scatter.1
where the time goes:
time: 516 us
  waiting for transfers between devices  432 us (84%)
  matrix products  30.7 us (6%)
  local copies, waits for them, and re-layouts  18 us (3%)
  between operations  13.3 us (3%)
  blocking collectives  12.4 us (2%)
  other arithmetic  8.83 us (2%)
    all_gather x1, waiting for transfers between devices, local(): qkv = add_rows(normed, lax.all_gather(w_qkv, 'seq', axis=0, tiled=True))  244 us
    all_gather x1, waiting for transfers between devices, local(): lax.all_gather(w_out, 'seq', axis=2, tiled=True)  74.5 us
    all_gather x1, waiting for transfers between devices, local(): lax.all_gather(value_rows, 'seq', axis=0, tiled=True)  50.1 us
    all_gather x1, waiting for transfers between devices, local(): lax.all_gather(key_rows, 'seq', axis=0, tiled=True)  32.4 us
    reduce_scatter x1, waiting for transfers between devices, local(): lax.psum_scatter(head_terms.astype(jnp.bfloat16), ('tp', 'sub'), scatter_...  30.8 us
    unnamed x22, local copies, waits for them, and re-layouts  15.1 us
    dot_general x1, matrix products, local(): jnp.einsum('the,hec->tc', attended, lax.all_gather(w_out, 'seq', axis=2,...  14.5 us
    all_gather x1, blocking collectives, local(): lax.all_gather(key_valid, 'seq', axis=0, tiled=True)  12.4 us
  transfers between devices with their start and end apart: 5, of which 5 were waited for; matrix products, arithmetic and copies ran while one was open for 3% of the time, Pallas kernels for 0%

commit v1 on v0

--- a/solution.py
+++ b/solution.py
@@ -6,6 +6,17 @@
 
 HD = 128
 TILE = 384
+
+
+def collect(shard, axis, dim):
+    ways = lax.axis_size(axis)
+    pieces = [shard]
+    for far in range(1, ways):
+        pieces.append(
+            lax.ppermute(pieces[far - 1], axis, [(d, (d - 1) % ways) for d in range(ways)])
+        )
+    line = jnp.concatenate(pieces, axis=dim)
+    return jnp.roll(line, lax.axis_index(axis) * shard.shape[dim], axis=dim)
 
 
 def modulate(latents, mod_shift, mod_scale):
@@ -86,7 +97,7 @@
         tile_rows,
         start_state,
         (
-            lax.all_gather(key_rows, "seq", axis=0, tiled=True),
+            collect(key_rows, "seq", 0),
             lax.all_gather(value_rows, "seq", axis=0, tiled=True),
             lax.all_gather(key_valid, "seq", axis=0, tiled=True),
         ),

time: 516 us -> 492 us (0.953)
  waiting for transfers between devices: 432 us -> 363 us
  blocking collectives: 12.4 us -> 48 us
  local copies, waits for them, and re-layouts: 18 us -> 24.9 us
    all_gather x1, waiting for transfers between devices: 74.5 us -> 0.02 us  [local(): lax.all_gather(w_out, 'seq', axis=2, tiled=True)]
    ppermute x0 -> x3, waiting for transfers between devices: none -> 59 us  [collect(): lax.ppermute(pieces[far - 1], axis, [(d, (d - 1) % ways) for d in range(w...]
    all_gather x1, blocking collectives: 12.4 us -> 48 us  [local(): lax.all_gather(key_valid, 'seq', axis=0, tiled=True)]
    all_gather x1 -> x0, waiting for transfers between devices: 32.4 us -> none  [local(): lax.all_gather(key_rows, 'seq', axis=0, tiled=True)]
    all_gather x1, waiting for transfers between devices: 50.1 us -> 27.9 us  [local(): lax.all_gather(value_rows, 'seq', axis=0, tiled=True)]
    unnamed x22 -> x30, local copies, waits for them, and re-layouts: 15.1 us -> 21.2 us
  transfers between devices with their start and end apart: 5 -> 7, of which waited for: 5 -> 5; matrix products, arithmetic and copies ran while one was open for 3% -> 8% of each run, Pallas kernels for 0% -> 0%
where the time goes in v1:
time: 492 us; the launch traced here: 491 us
  waiting for transfers between devices  363 us (74%)
  blocking collectives  48 us (10%)
  matrix products  31.9 us (6%)
  local copies, waits for them, and re-layouts  24.9 us (5%)
  between operations  13.4 us (3%)
  other arithmetic  9.42 us (2%)
    all_gather x1, waiting for transfers between devices, local(): qkv = add_rows(normed, lax.all_gather(w_qkv, 'seq', axis=0, tiled=True))  245 us
    ppermute x3, waiting for transfers between devices, collect(): lax.ppermute(pieces[far - 1], axis, [(d, (d - 1) % ways) for d in range(w...  59 us
    all_gather x1, blocking collectives, local(): lax.all_gather(key_valid, 'seq', axis=0, tiled=True)  48 us
    reduce_scatter x1, waiting for transfers between devices, local(): lax.psum_scatter(head_terms.astype(jnp.bfloat16), ('tp', 'sub'), scatter_...  30.8 us
    all_gather x1, waiting for transfers between devices, local(): lax.all_gather(value_rows, 'seq', axis=0, tiled=True)  27.9 us
    unnamed x30, local copies, waits for them, and re-layouts  21.2 us
    dot_general x1, matrix products, local(): jnp.einsum('the,hec->tc', attended, lax.all_gather(w_out, 'seq', axis=2,...  14.5 us
    unnamed x1, matrix products  10.7 us
  transfers between devices with their start and end apart: 7, of which 5 were waited for; matrix products, arithmetic and copies ran while one was open for 8% of the time, Pallas kernels for 0%

profile of v1, /device:TPU:0, one launch (start us, length us, event | category | flops | bytes accessed | tf_op | source)
XLA Modules:
  0.0 491.4 jit_solution(7662756561688399352)
XLA Ops:
  6.5 0.0 copy-start.1
  6.5 0.0 all-gather.6.cloned.1.call-start
  6.5 6.2 %copy.22 = bf16[768,3,6,128]{0,3,2,1:T(8,128)(2,1)} copy(bf16[768,3,6,128]{3,0,2,1:T(8,128)(2,1)} %param.12) | data formatting | bytes 7077888 | tf_op args[1]
  12.7 0.0 copy-start.4
  12.7 0.0 copy-start.8
  12.7 0.0 all-gather.6.cloned.1.call-update
  12.8 0.0 all-gather.8.cloned.1.call-start
  12.8 0.7 all-gather.8.cloned.1.call-update
  13.5 0.0 all-gather.10.cloned.1.call-start
  13.6 0.0 copy-done.1
  13.6 0.4 convert_reduce_fusion
  14.0 0.8 fusion.8
  14.7 0.0 copy-done.4
  14.8 244.8 %all-gather.6.cloned.1.call-done = bf16[3072,3,6,128]{0,3,2,1:T(8,128)(2,1)} async-done(((bf16[768,3,6,128]{0,3,2,1:T(8,128)(2,1)}), bf16[3072,3,6,128]{0,3,2,1:T(8,128)(2,1)}) %all-gather.6.cloned.1.call-update) | async-done | bytes 14155792 | tf_op jit(solution)/shard_map/all_gather | solution.py:81
  259.5 0.0 copy-done.8
  259.5 0.0 copy-start.7
  259.5 10.7 %fusion.13 = f32[384,2304]{0,1:S(1)} fusion(bf16[3072,2304]{0,1:T(8,128)(2,1)} %bitcast.46, bf16[384,3072]{1,0:T(8,128)(2,1)S(1)} %copy-done.1, f32[3072]{0:T(1024)S(1)} %copy-done.8, f32[3072]{0:T(1024)S(1)} %broadcast_add_fusion, f32[384]{0:T(512)S(1)} %add_rsqrt_fusion.2, f32[384]{0:T(512)S(1)} %broadcast_multiply_fusion), kind=kOutput, calls=%fused_computation.18 | convolution fusion | flops 5442895872 | bytes 20081664
  270.2 0.0 copy-start.2
  270.3 0.0 copy-start.5
  270.3 0.0 copy-start.9
  270.3 0.0 copy-start.10
  270.3 0.2 multiply_reduce_fusion.1
  270.5 0.0 copy-done.7
  270.5 1.6 constant_dynamic-update-slice_fusion.7
  272.1 0.0 copy-start.3
  272.1 0.3 collective-permute-start
  272.4 42.0 %collective-permute-done = bf16[384,6,128]{0,2,1:T(8,128)(2,1)S(1)} collective-permute-done((bf16[384,6,128]{0,2,1:T(8,128)(2,1)S(1)}, bf16[384,6,128]{0,2,1:T(8,128)(2,1)S(1)}, u32[]{:S(2)}, u32[]{:S(2)}) %collective-permute-start) | collective-permute-done | bytes 589856 | tf_op jit(solution)/shard_map/ppermute | solution.py:16
  314.3 0.0 copy-done.3
  314.3 0.0 collective-permute-start.1
  314.3 0.0 copy-done.5
  314.3 48.0 %all-gather.1 = s32[4,1,384]{2,1,0:T(1,128)S(1)} all-gather(s32[1,1,384]{2,1,0:T(1,128)S(1)} %reshape.138), channel_id=1, replica_groups=mesh['rep'=2,'seq'=4,'tp'=2,'sub'=2] {'seq'}, dimensions={0}, use_global_device_ids=true | all-gather | bytes 7680 | tf_op jit(solution)/shard_map/all_gather | solution.py:102
  362.4 0.0 copy-done.9
  362.4 0.0 copy-done.2
  362.4 0.9 slice.28
  363.3 0.0 all-gather.10.cloned.1.call-update
  363.4 0.0 reduce-scatter.2.cloned.1.call-start
  363.4 0.0 copy-done.10
  363.4 0.1 fusion.44
  363.6 0.0 collective-permute-done.1
  363.6 0.2 collective-permute-start.2
  363.8 0.5 fusion.12
  364.4 0.0 copy-start.6
  364.4 1.0 constant_dynamic-update-slice_fusion.6
  365.4 2.0 constant_dynamic-update-slice_fusion.5
  367.4 17.0 %collective-permute-done.2 = bf16[384,6,128]{0,2,1:T(8,128)(2,1)} collective-permute-done((bf16[384,6,128]{0,2,1:T(8,128)(2,1)}, bf16[384,6,128]{0,2,1:T(8,128)(2,1)}, u32[]{:S(2)}, u32[]{:S(2)}) %collective-permute-start.2) | collective-permute-done | bytes 589856 | tf_op jit(solution)/shard_map/ppermute | solution.py:16
  384.4 2.0 constant_dynamic-update-slice_fusion.4
  386.4 2.0 constant_dynamic-update-slice_fusion.3
  388.4 0.9 constant_dynamic-update-slice_fusion.2
  389.4 2.0 constant_dynamic-update-slice_fusion.1
  391.4 2.0 constant_dynamic-update-slice_fusion
  393.4 0.0 copy-done.6
  393.4 6.2 %fusion = (f32[6,384]{1,0:T(8,128)S(1)}, f32[6,384,1536]{2,1,0:T(8,128)S(1)}) fusion(pred[384,1536]{1,0:T(8,128)(4,1)S(1)} %fusion.12, bf16[3072,6,128]{0,2,1:T(8,128)(2,1)} %constant_dynamic-update-slice_fusion, s32[]{:T(128)S(6)} %select_n.36, f32[384,3,6,128]{0,3,2,1:T(8,128)} %bitcast.44, f32[128]{0:T(128)S(1)} %copy-done.6, ...), kind=kOutput, calls=%fused_computation.2 | convolution fusion | flops 917468928 | bytes 18303492 | tf_op jit(solution)/shard_map/qhe,khe->hqk/dot_general | solution.py:51
  399.6 0.0 copy-start
  399.6 5.0 %copy-done = f32[6,384,1536]{2,1,0:T(8,128)} copy-done((f32[6,384,1536]{2,1,0:T(8,128)}, f32[6,384,1536]{2,1,0:T(8,128)S(1)}, u32[]{:S(2)}) %copy-start) | copy-done | bytes 14155800
  404.7 4.2 fusion.1
  408.9 0.0 all-gather.8.cloned.1.call-done
  408.9 27.9 %all-gather.10.cloned.1.call-done = bf16[1536,1,6,128]{0,3,2,1:T(8,128)(2,1)} async-done(((bf16[384,1,6,128]{0,3,2,1:T(8,128)(2,1)}), bf16[1536,1,6,128]{0,3,2,1:T(8,128)(2,1)}) %all-gather.10.cloned.1.call-update) | async-done | bytes 2359312 | tf_op jit(solution)/shard_map/all_gather | solution.py:101
  436.8 14.5 %bitcast_convert_fusion = bf16[384,3072]{1,0:T(8,128)(2,1)} fusion(bf16[6,128,3072]{2,1,0:T(8,128)(2,1)} %all-gather.8.cloned.1.call-done, f32[6,384,1536]{2,1,0:T(8,128)} %copy-done, f32[6,384]{1,0:T(8,128)S(1)} %broadcast_maximum_fusion, pred[384,1536]{1,0:T(8,128)(4,1)S(1)} %fusion.12, bf16[1536,1,6,128]{0,3,2,1:T(8,128)(2,1)} %all-gather.10.cloned.1.call-done, ...), kind=kOutput, calls=%fused_computation.15 | convolution fusion | flops 2737373184 | bytes 24201216 | tf_op jit(solution)/shard_map/the,hec->tc/dot_general | solution.py:106
  451.3 0.0 reduce-scatter.2.cloned.1.call-update
  451.3 0.8 dynamic_slice.11
  452.1 30.8 %reduce-scatter.2.cloned.1.call-done = bf16[384,768]{1,0:T(8,128)(2,1)} async-done(((bf16[384,3072]{1,0:T(8,128)(2,1)}), bf16[384,768]{1,0:T(8,128)(2,1)}) %reduce-scatter.2.cloned.1.call-update) | async-done | bytes 589840 | tf_op jit(solution)/shard_map/reduce_scatter | solution.py:112
  482.8 2.1 add_convert_fusion
  (12 shorter events, 0.1 us)
Async XLA Ops:
  6.5 7.0 %copy-start.1 = (bf16[384,3072]{1,0:T(8,128)(2,1)S(1)}, bf16[384,3072]{1,0:T(8,128)(2,1)}, u32[]{:S(2)}) copy-start(bf16[384,3072]{1,0:T(8,128)(2,1)} %param.11) | copy-start | bytes 7077892
  6.5 253.0 %all-gather.6.cloned.1.call-start = ((), (), s32[]{:S(2)}) async-start(), calls=%async_computation.1 | async-start | bytes 17694720 | tf_op jit(solution)/shard_map/all_gather | solution.py:81
  12.7 2.0 copy-start.4
  12.7 246.8 %copy-start.8 = (f32[3072]{0:T(1024)S(1)}, f32[3072]{0:T(1024)}, u32[]{:S(2)}) copy-start(f32[3072]{0:T(1024)} %param.16) | copy-start | bytes 36868
  12.8 396.2 %all-gather.8.cloned.1.call-start = ((), (), s32[]{:S(2)}) async-start(), calls=%async_computation.2 | async-start | bytes 5898240 | tf_op jit(solution)/shard_map/all_gather | solution.py:109
  13.5 423.3 %all-gather.10.cloned.1.call-start = ((), (), s32[]{:S(2)}) async-start(), calls=%async_computation.4 | async-start | bytes 2949120 | tf_op jit(solution)/shard_map/all_gather | solution.py:101
  259.5 11.0 %copy-start.7 = (f32[128]{0:T(128)S(1)}, f32[128]{0:T(128)}, u32[]{:S(2)}) copy-start(f32[128]{0:T(128)} %param.15) | copy-start | bytes 1540
  270.2 92.2 %copy-start.2 = (f32[384,2304]{0,1}, f32[384,2304]{0,1:S(1)}, u32[]{:S(2)}) copy-start(f32[384,2304]{0,1:S(1)} %fusion.13) | copy-start | bytes 10616836
  270.3 44.1 %copy-start.5 = (s32[384]{0:T(512)S(1)}, s32[384]{0:T(512)}, u32[]{:S(2)}) copy-start(s32[384]{0:T(512)} %param.21) | copy-start | bytes 4612
  270.3 92.1 %copy-start.9 = (s32[1,9]{1,0:T(1,128)S(1)}, s32[1,9]{1,0:T(1,128)}, u32[]{:S(2)}) copy-start(s32[1,9]{1,0:T(1,128)} %param.20) | copy-start | bytes 112
  270.3 93.1 %copy-start.10 = (s32[1,9]{1,0:T(1,128)S(1)}, s32[1,9]{1,0:T(1,128)}, u32[]{:S(2)}) copy-start(s32[1,9]{1,0:T(1,128)} %param.19) | copy-start | bytes 112
  272.1 42.2 %copy-start.3 = (bf16[384,6,128]{0,2,1:T(8,128)(2,1)}, bf16[384,6,128]{0,2,1:T(8,128)(2,1)S(1)}, u32[]{:S(2)}) copy-start(bf16[384,6,128]{0,2,1:T(8,128)(2,1)S(1)} %get-tuple-element.8) | copy-start | bytes 1769476
  272.1 42.2 %collective-permute-start = (bf16[384,6,128]{0,2,1:T(8,128)(2,1)S(1)}, bf16[384,6,128]{0,2,1:T(8,128)(2,1)S(1)}, u32[]{:S(2)}, u32[]{:S(2)}) collective-permute-start(bf16[384,6,128]{0,2,1:T(8,128)(2,1)S(1)} %get-tuple-element.8), channel_id=1, source_target_pairs={{0,12},{4,0},{8,4},{12,8},{1,13},{5,1},{9,5},{13,9},{2,14},{6,2},{... | collective-permute-start | bytes 1769480 | tf_op jit(solution)/shard_map/ppermute | solution.py:16
  314.3 49.2 %collective-permute-start.1 = (bf16[384,6,128]{0,2,1:T(8,128)(2,1)S(1)}, bf16[384,6,128]{0,2,1:T(8,128)(2,1)}, u32[]{:S(2)}, u32[]{:S(2)}) collective-permute-start(bf16[384,6,128]{0,2,1:T(8,128)(2,1)S(1)} %collective-permute-done), channel_id=1, source_target_pairs={{0,12},{4,0},{8,4},{12,8},{1,13},{5,1},{9,5},{13,9},{2,14},{6,2},{... | collective-permute-start | bytes 1769480 | tf_op jit(solution)/shard_map/ppermute | solution.py:16
  363.4 119.5 %reduce-scatter.2.cloned.1.call-start = ((), (), s32[]{:S(2)}) async-start(), calls=%async_computation.3 | async-start | bytes 2949120 | tf_op jit(solution)/shard_map/reduce_scatter | solution.py:112
  363.6 20.8 %collective-permute-start.2 = (bf16[384,6,128]{0,2,1:T(8,128)(2,1)}, bf16[384,6,128]{0,2,1:T(8,128)(2,1)}, u32[]{:S(2)}, u32[]{:S(2)}) collective-permute-start(bf16[384,6,128]{0,2,1:T(8,128)(2,1)} %collective-permute-done.1), channel_id=1, source_target_pairs={{0,12},{4,0},{8,4},{12,8},{1,13},{5,1},{9,5},{13,9},{2,14},{6,2},{... | collective-permute-start | bytes 1769480 | tf_op jit(solution)/shard_map/ppermute | solution.py:16
  364.4 29.0 %copy-start.6 = (f32[128]{0:T(128)S(1)}, f32[128]{0:T(128)}, u32[]{:S(2)}) copy-start(f32[128]{0:T(128)} %param.14) | copy-start | bytes 1540
  399.6 5.1 %copy-start = (f32[6,384,1536]{2,1,0:T(8,128)}, f32[6,384,1536]{2,1,0:T(8,128)S(1)}, u32[]{:S(2)}) copy-start(f32[6,384,1536]{2,1,0:T(8,128)S(1)} %get-tuple-element.10) | copy-start | bytes 42467332
Sparse Core Ops, SparseCore 0:
  12.9 246.6 all-gather.5
  261.1 117.4 all-gather.7
  380.2 56.4 all-gather.9
  451.4 31.4 reduce-scatter.1
